TPU v7x, 32 devices: a whole 2x2x4 slice. The times are simulated.
32 devices in a mesh: path: 2 (over x), mesh: 2 (over y), grid: 8 (over z, core).
Axes of the slice: x: 2, y: 2, z: 4, core: 2. Of those that a mesh axis runs over, the one named last changes fastest.
Arguments:
- path_bands: float32 [2, 16, 64, 64, 128], P('path', None, 'grid'), may hold values from -6 to 6
- occupied: float32 [2, 1, 64, 64, 128], P('mesh', None, 'grid', 'path'), may hold values from -6 to 6
- path_kpts: int32 [2, 3], P('path'), may hold values from 0 to 7
- mesh_kpts: int32 [2, 3], replicated, may hold values from 0 to 7
- mesh_shift: int32 [2, 3], replicated, may hold values from -1 to 1
Outputs:
- applied: float32 [2, 16, 64, 64, 128], P('path', 'mesh', 'grid')
- intersection: float32 [2, 2, 16, 16], P('path')
All inputs are finite; a program needn't handle non-finite values.
Results may differ from a plain program's by a relative error of at most 0.0001.
Values sent between devices are 32-bit elements; how exact they have to be, the bound alone decides.
No kernel may reach another device: no remote copies, remote signals or barrier semaphores. Data moves between devices by JAX's collectives and lax.ppermute only.
A program may use at most 64 MiB of HBM per device.

v0:
```python
import math

import jax
import jax.numpy as jnp
import ml_dtypes
import numpy as np
from jax import lax
from jax.experimental import pallas as pl
from jax.experimental.pallas import tpu as pltpu
from jax.sharding import PartitionSpec as P

KDIV = 8


BOX_LENGTH = 42.7
SCREEN_SQ = 0.04
MIXING = 0.25
HIGHEST_PRECISION = lax.Precision.HIGHEST


def signed_frequencies(indices, points):
    return (indices + points // 2) % points - points // 2


def dft_tables(positions, points):
    freqs = jnp.arange(points, dtype=jnp.int32)
    product = positions[:, None] * freqs[None, :] % points
    angles = 2.0 * math.pi / points * product.astype(jnp.float32)
    return (jnp.cos(angles), jnp.sin(angles))


def last_matrix(points, inverse):
    cosine_table, sine_table = dft_tables(jnp.arange(points, dtype=jnp.int32), points)
    if inverse:
        upper = jnp.concatenate([cosine_table, sine_table], 1)
        lower = jnp.concatenate([-sine_table, cosine_table], 1)
    else:
        upper = jnp.concatenate([cosine_table, -sine_table], 1)
        lower = jnp.concatenate([sine_table, cosine_table], 1)
    return jnp.concatenate([upper, lower], 0)


def along_axis(values, cosine_table, sine_table, contract_dim, inverse):
    letters = "abcde"
    form = (
        letters
        + ","
        + letters[contract_dim]
        + "w->"
        + letters[:contract_dim]
        + "w"
        + letters[contract_dim + 1 :]
    )
    cos_part = jnp.einsum(form, values, cosine_table, precision=HIGHEST_PRECISION)
    sin_part = jnp.einsum(form, values, sine_table, precision=HIGHEST_PRECISION)
    half_width = values.shape[-1] // 2
    sin_real = sin_part[..., :half_width]
    sin_imag = sin_part[..., half_width:]
    if inverse:
        return cos_part + jnp.concatenate([-sin_imag, sin_real], -1)
    return cos_part + jnp.concatenate([sin_imag, -sin_real], -1)


def rotate_orbitals(orbitals, shifts, x_planes):
    points = orbitals.shape[3]
    coords = jnp.arange(points, dtype=jnp.int32)
    product = (
        shifts[:, 0][:, None, None, None] * x_planes[None, :, None, None]
        + shifts[:, 1][:, None, None, None] * coords[None, None, :, None]
        + shifts[:, 2][:, None, None, None] * coords[None, None, None, :]
    ) % points
    angles = 2.0 * math.pi / points * product.astype(jnp.float32)
    cosines = jnp.cos(angles)[:, None]
    sines = jnp.sin(angles)[:, None]
    real_part = orbitals[..., :points]
    imag_part = orbitals[..., points:]
    return jnp.concatenate(
        [real_part * cosines - imag_part * sines, real_part * sines + imag_part * cosines], -1
    )


def pair_fields(rotated, band_fields):
    points = band_fields.shape[2]
    rot_real = rotated[..., :points][:, :, None]
    rot_imag = rotated[..., points:][:, :, None]
    band_real = band_fields[..., :points][None, None]
    band_imag = band_fields[..., points:][None, None]
    pairs = jnp.concatenate(
        [rot_real * band_real + rot_imag * band_imag, rot_real * band_imag - rot_imag * band_real],
        -1,
    )
    return pairs.reshape(
        (rotated.shape[0], rotated.shape[1] * band_fields.shape[0]) + band_fields.shape[1:]
    )


def accumulate(rotated, potential, nbands):
    points = rotated.shape[3]
    shaped = potential.reshape((rotated.shape[0], rotated.shape[1], nbands) + potential.shape[2:])
    rot_real = rotated[..., :points][:, :, None]
    rot_imag = rotated[..., points:][:, :, None]
    pot_real = shaped[..., :points]
    pot_imag = shaped[..., points:]
    summed = jnp.concatenate(
        [
            jnp.sum(rot_real * pot_real - rot_imag * pot_imag, axis=(0, 1)),
            jnp.sum(rot_real * pot_imag + rot_imag * pot_real, axis=(0, 1)),
        ],
        -1,
    )
    return -MIXING * summed


def intersection_part(band_fields, applied):
    points = band_fields.shape[2]
    nbands = band_fields.shape[0]
    band_real = band_fields[..., :points].reshape(nbands, -1)
    band_imag = band_fields[..., points:].reshape(nbands, -1)
    app_real = applied[..., :points].reshape(applied.shape[0], -1)
    app_imag = applied[..., points:].reshape(applied.shape[0], -1)
    real_sum = jnp.dot(band_real, app_real.T, precision=HIGHEST_PRECISION) + jnp.dot(
        band_imag, app_imag.T, precision=HIGHEST_PRECISION
    )
    imag_sum = jnp.dot(band_real, app_imag.T, precision=HIGHEST_PRECISION) - jnp.dot(
        band_imag, app_real.T, precision=HIGHEST_PRECISION
    )
    return jnp.stack([real_sum, imag_sum]) / float(points**3)


def screened_kernel(path_point, mesh_points, y_rows, points):
    offset_frac = (path_point[None, :] - mesh_points).astype(jnp.float32) / KDIV
    all_freqs = signed_frequencies(jnp.arange(points, dtype=jnp.int32), points).astype(jnp.float32)
    row_freqs = signed_frequencies(y_rows, points).astype(jnp.float32)
    square_x = (all_freqs[None, :] + offset_frac[:, 0:1]) ** 2
    square_y = (row_freqs[None, :] + offset_frac[:, 1:2]) ** 2
    square_z = (all_freqs[None, :] + offset_frac[:, 2:3]) ** 2
    squares = square_x[:, :, None, None] + square_y[:, None, :, None] + square_z[:, None, None, :]
    kernel = (
        4.0 * math.pi / ((2.0 * math.pi / BOX_LENGTH) ** 2 * squares + SCREEN_SQ) / float(points**3)
    )
    return jnp.concatenate([kernel, kernel], -1)


def spread_per_device(path_bands, occupied, path_kpts, mesh_kpts, mesh_shift):
    points = path_bands.shape[3]
    nbands = path_bands.shape[1]
    local_planes = path_bands.shape[2]
    grid_count = lax.axis_size("grid")
    mesh_count = lax.axis_size("mesh")
    grid_index = lax.axis_index("grid")
    mesh_index = lax.axis_index("mesh")
    whole_orbitals = lax.all_gather(occupied, "path", axis=3, tiled=True)
    forward_z = last_matrix(points, False)
    inverse_z = last_matrix(points, True)
    cos_y, sin_y = dft_tables(jnp.arange(points, dtype=jnp.int32), points)
    band_all = path_bands[0]
    path_point = path_kpts[0]
    share_planes = local_planes // mesh_count
    both_orbitals = lax.all_to_all(whole_orbitals, "mesh", split_axis=2, concat_axis=0, tiled=True)
    x_planes = (
        grid_index * local_planes
        + mesh_index * share_planes
        + jnp.arange(share_planes, dtype=jnp.int32)
    )
    rotated = rotate_orbitals(both_orbitals, mesh_shift, x_planes)
    band_mine = lax.dynamic_slice_in_dim(band_all, mesh_index * share_planes, share_planes, 1)
    values = pair_fields(rotated, band_mine)
    values = jnp.matmul(values, forward_z, precision=HIGHEST_PRECISION)
    pair_field = along_axis(values, cos_y, sin_y, 3, False)
    wide_count = mesh_count * grid_count
    rows_y = points // wide_count
    flat_index = mesh_index * grid_count + grid_index
    y_rows = flat_index * rows_y + jnp.arange(rows_y, dtype=jnp.int32)
    kernel = screened_kernel(path_point, mesh_kpts, y_rows, points)
    positions = jnp.arange(points, dtype=jnp.int32)
    piece_index = positions // share_planes
    plane_index = (
        piece_index % grid_count * local_planes
        + piece_index // grid_count * share_planes
        + positions % share_planes
    )
    cos_x, sin_x = dft_tables(plane_index, points)
    moved = (
        along_axis(
            lax.all_to_all(pair_field, ("mesh", "grid"), split_axis=3, concat_axis=2, tiled=True),
            cos_x,
            sin_x,
            2,
            False,
        )
        * kernel[:, None]
    )
    moved = along_axis(moved, cos_x.T, sin_x.T, 2, True)
    potential = lax.all_to_all(moved, ("mesh", "grid"), split_axis=2, concat_axis=3, tiled=True)
    values = potential
    values = along_axis(values, cos_y, sin_y, 3, True)
    applied = accumulate(
        rotated, jnp.matmul(values, inverse_z, precision=HIGHEST_PRECISION), nbands
    )
    partial_value = intersection_part(band_mine, applied)
    result_bands = lax.all_to_all(applied, "mesh", split_axis=0, concat_axis=1, tiled=True)
    intersection = lax.psum(partial_value, ("mesh", "grid"))
    return (result_bands[None], intersection[None])


def split_table(table):
    high = table.astype(ml_dtypes.bfloat16)
    low = (table - high.astype(np.float64)).astype(ml_dtypes.bfloat16)
    return high, low


def transform_tables(points):
    index = np.arange(points)
    angles = 2.0 * np.pi * ((index[:, None] * index[None, :]) % points) / points
    cos, sin = np.cos(angles), np.sin(angles)
    zero = np.zeros_like(cos)
    last_forward = np.block([[cos, zero, -sin, zero], [sin, zero, cos, zero], [zero, cos, zero, -sin], [zero, sin, zero, cos]])
    last_inverse = np.block([[cos, sin, zero, zero], [zero, zero, cos, sin], [-sin, cos, zero, zero], [zero, zero, -sin, cos]])
    row_forward = np.block([[cos, sin], [-sin, cos]])
    row_inverse = np.block([[cos, -sin], [sin, cos]])
    last = []
    for table in (last_forward, last_inverse):
        last.extend(split_table(table))
    rows = []
    for table in (row_forward, row_inverse):
        high, low = split_table(table)
        rows.append(np.block([[high, high], [low, np.zeros_like(low)]]).astype(ml_dtypes.bfloat16))
    half = points // 2
    turn = 2.0 * np.pi * np.arange(half) / points
    ones = np.ones((half, points))
    twiddle = np.stack([np.concatenate([ones, ones * np.cos(turn)[:, None]], 1), np.concatenate([0 * ones, ones * np.sin(turn)[:, None]], 1)])
    return last, rows, twiddle.astype(np.float32)


def split_values(values):
    high = values.astype(jnp.bfloat16)
    low = (values - high.astype(jnp.float32)).astype(jnp.bfloat16)
    return high, low


def fft_list(real, imag):
    size = len(real)
    if size == 1:
        return real, imag
    half = size // 2
    even_r, even_i = fft_list(real[0::2], imag[0::2])
    odd_r, odd_i = fft_list(real[1::2], imag[1::2])
    out_r, out_i = [None] * size, [None] * size
    root = math.sqrt(0.5)
    for k in range(half):
        r, i = odd_r[k], odd_i[k]
        if k == 0:
            tr, ti = r, i
        elif 4 * k == size:
            tr, ti = i, -r
        elif 8 * k == size:
            tr, ti = (r + i) * root, (i - r) * root
        elif 8 * k == 3 * size:
            tr, ti = (i - r) * root, (r + i) * (-root)
        else:
            c, s = math.cos(2 * math.pi * k / size), math.sin(2 * math.pi * k / size)
            tr, ti = r * c + i * s, i * c - r * s
        if 4 * k == size:
            out_r[k], out_i[k] = even_r[k] + i, even_i[k] - r
            out_r[k + half], out_i[k + half] = even_r[k] - i, even_i[k] + r
        else:
            out_r[k], out_i[k] = even_r[k] + tr, even_i[k] + ti
            out_r[k + half], out_i[k + half] = even_r[k] - tr, even_i[k] - ti
    return out_r, out_i


def f32dot(a, b):
    return jnp.dot(a, b, preferred_element_type=jnp.float32)


def pair_kernel(spots_ref, *refs):
    nz = 4
    mine, other = refs[:nz], refs[nz : 2 * nz]
    first_own, first_far, second_kept, second_crossed = refs[2 * nz : 2 * nz + 4]
    kern_ref, table_ref, tw_ref = refs[2 * nz + 4 : 2 * nz + 7]
    lfh, lfl, lih, lil, rf, ri = [table_ref.at[at] for at in range(6)]
    keep, send = refs[2 * nz + 7 : 3 * nz + 7], refs[3 * nz + 7 : 4 * nz + 7]
    vre, vim = refs[4 * nz + 7 :]
    share, rows, lanes = mine[0].shape
    points = rows
    half_z = nz // 2
    z, core, path = spots_ref[0], spots_ref[1], spots_ref[2]
    low = lax.broadcasted_iota(jnp.int32, (rows, lanes), 1) < points
    step = 4

    def swap(v):
        return pltpu.roll(v, points, v.ndim - 1)

    def orbital(d, parity, i):
        if d < half_z:
            own, far = first_own[parity, d, i], first_far[parity, d, i]
        else:
            ref = second_crossed if parity else second_kept
            own, far = ref[0, d - half_z, i], ref[1, d - half_z, i]
        r = jnp.concatenate([jnp.where(path == 0, own, far), jnp.where(path == 0, far, own)], 0)
        s = swap(r)
        return jnp.where(low, r, s), jnp.where(low, s, -r)

    def place(d, parity, part):
        side = core if parity == 0 else 1 - core
        return share * (2 * ((z ^ d) & 1) + side) + part * step

    def forward(d, parity, part):
        first = place(d, parity, part)
        halves = []
        for at in (d, d ^ half_z):
            planes = []
            for i in range(step):
                real, imag = orbital(at, parity, part * step + i)
                band = (other if parity else mine)[at][part * step + i]
                planes.append(real * band + imag * swap(band))
            halves.append(jnp.concatenate(planes, 0))
        hi, lo = split_values(jnp.concatenate(halves, 1))
        u = f32dot(hi, lfh[...]) + f32dot(lo, lfh[...]) + f32dot(hi, lfl[...])
        uh, ul = split_values(u)
        for i in range(0, step, 2):

            def stack(v):
                cols = []
                for j in (0, 1):
                    plane = v[(i + j) * rows : (i + j + 1) * rows]
                    cols.append(jnp.concatenate([plane[:, :lanes], plane[:, lanes:]], 0))
                return jnp.concatenate(cols, 1)

            d2 = f32dot(rf[...], jnp.concatenate([stack(uh), stack(ul)], 0))
            v = d2[: 2 * rows] + d2[2 * rows :]
            for j in (0, 1):
                vre[first + i + j] = v[:rows, j * lanes : (j + 1) * lanes]
                vim[first + i + j] = v[rows:, j * lanes : (j + 1) * lanes]

    def inverse(d, parity, part):
        first = place(d, parity, part)
        res = []
        for i in range(0, step, 2):
            cols = []
            for j in (0, 1):
                rh, rl = split_values(vre[first + i + j])
                ih, il = split_values(vim[first + i + j])
                cols.append(jnp.concatenate([rh, ih, rl, il], 0))
            d2 = f32dot(ri[...], jnp.concatenate(cols, 1))
            u = d2[: 2 * rows] + d2[2 * rows :]
            for j in (0, 1):
                plane = u[:, j * lanes : (j + 1) * lanes]
                res.append(jnp.concatenate([plane[:rows], plane[rows:]], 1))
        hi, lo = split_values(jnp.concatenate(res, 0))
        p = f32dot(hi, lih[...]) + f32dot(lo, lih[...]) + f32dot(hi, lil[...])
        for i in range(step):
            for side, at in enumerate((d, d ^ half_z)):
                real, imag = orbital(at, parity, part * step + i)
                pot = p[i * rows : (i + 1) * rows, side * lanes : (side + 1) * lanes]
                out = send if parity else keep
                out[at][part * step + i] = real * pot - imag * swap(pot)

    def each_part(work):
        def body(part, carry):
            for d in range(half_z):
                for parity in (0, 1):
                    work(d, parity, part)
            return carry

        lax.fori_loop(0, share // step, body, 0)

    each_part(forward)

    n = vre.shape[0]
    sub = 8
    sign = jnp.where(low[:sub], 1.0, -1.0).astype(jnp.float32)

    def x_body(t, carry):
        sl = pl.ds(pl.multiple_of(t * sub, sub), sub)
        re, im = [], []
        for x in range(n):
            a, b = vre[x, sl, :], vim[x, sl, :]
            a = a * sign + swap(a)
            b = b * sign + swap(b)
            if x:
                c, s = tw_ref[0, x : x + 1, :], tw_ref[1, x : x + 1, :]
                a, b = a * c + b * s, b * c - a * s
            re.append(a)
            im.append(b)
        re, im = fft_list(re, im)
        for x in range(n):
            k = kern_ref[x, sl, :]
            re[x] = re[x] * k
            im[x] = im[x] * k
        im, re = fft_list(im, re)
        for x in range(n):
            a, b = re[x], im[x]
            if x:
                c, s = tw_ref[0, x : x + 1, :], tw_ref[1, x : x + 1, :]
                a, b = a * c - b * s, b * c + a * s
            vre[x, sl, :] = a * sign + swap(a)
            vim[x, sl, :] = b * sign + swap(b)
        return carry

    lax.fori_loop(0, rows // sub, x_body, 0)
    each_part(inverse)


def apply_pair(spots, mine, other, orbital, kern):
    share, rows, lanes = mine[0].shape
    last, row, tw = transform_tables(rows)
    shape = jax.ShapeDtypeStruct(mine[0].shape, jnp.float32)
    vm = pl.BlockSpec(memory_space=pltpu.VMEM)
    operands = [*mine, *other, *orbital, kern, np.stack(last + row), tw]
    count = len(mine)
    outs = pl.pallas_call(
        pair_kernel,
        out_shape=(shape,) * (2 * count),
        in_specs=[pl.BlockSpec(memory_space=pltpu.SMEM)] + [vm] * len(operands),
        out_specs=(vm,) * (2 * count),
        scratch_shapes=[pltpu.VMEM((count * share, rows, lanes), jnp.float32)] * 2,
        cost_estimate=pl.CostEstimate(
            flops=2 * 10**9, bytes_accessed=7 * 2**20, transcendentals=0
        ),
        compiler_params=pltpu.CompilerParams(vmem_limit_bytes=30 * 2**20),
        name="pair",
    )(spots, *operands)
    return outs[:count], outs[count:]


LANES = 128


def intersect_kernel(slot_ref, bands_ref, chunk_ref, before_ref, out_ref, turned, sums):
    nbands, cells, lanes = bands_ref.shape
    sub, group = 8, 8
    low = lax.broadcasted_iota(jnp.int32, (cells, lanes), 1) < lanes // 2
    rolled = pltpu.roll(chunk_ref[...], lanes // 2, 1)
    turned[...] = jnp.where(low, rolled, -rolled)
    for first in range(0, nbands, group):

        def body(t, acc):
            sl = pl.ds(pl.multiple_of(t * sub, sub), sub)
            real, imag = chunk_ref[sl, :], turned[sl, :]
            out = []
            for a in range(group):
                band = bands_ref[first + a, sl, :]
                out.append(acc[2 * a] + band * real)
                out.append(acc[2 * a + 1] + band * imag)
            return tuple(out)

        zero = jnp.zeros((sub, lanes), jnp.float32)
        acc = lax.fori_loop(0, cells // sub, body, (zero,) * (2 * group), unroll=4)
        for a in range(group):
            sums[first + a] = acc[2 * a]
            sums[nbands + first + a] = acc[2 * a + 1]
    column = lax.broadcasted_iota(jnp.int32, out_ref.shape, 1)
    value = jnp.sum(jnp.sum(sums[...], axis=1), axis=1, keepdims=True)
    out_ref[...] = before_ref[...] + jnp.where(column == slot_ref[0], value, 0.0)


def intersect(slot, bands, chunk, before):
    nbands, lanes = bands.shape[0], bands.shape[-1]
    bands = bands.reshape(nbands, -1, lanes)
    chunk = chunk.reshape(-1, lanes)
    vm = pl.BlockSpec(memory_space=pltpu.VMEM)
    return pl.pallas_call(
        intersect_kernel,
        out_shape=jax.ShapeDtypeStruct((2 * nbands, lanes), jnp.float32),
        in_specs=[pl.BlockSpec(memory_space=pltpu.SMEM), vm, vm, vm],
        out_specs=vm,
        scratch_shapes=[
            pltpu.VMEM(chunk.shape, jnp.float32),
            pltpu.VMEM((2 * nbands, 8, lanes), jnp.float32),
        ],
        cost_estimate=pl.CostEstimate(flops=10**7, bytes_accessed=4 * 2**20, transcendentals=0),
        compiler_params=pltpu.CompilerParams(vmem_limit_bytes=12 * 2**20),
        name="intersect",
    )(slot, bands, chunk, before)


def owner_kernel_values(path_point, mesh_point, shift, points):
    half = points // 2
    offset = (path_point - mesh_point).astype(jnp.float32) / KDIV
    lane = jnp.arange(2 * points, dtype=jnp.int32)

    def square(indices, axis):
        freqs = signed_frequencies(indices - shift[axis], points).astype(jnp.float32)
        return (freqs + offset[axis]) ** 2

    x_index = 2 * jnp.arange(half, dtype=jnp.int32)[:, None] + lane[None, :] // points
    plane = square(x_index, 0) + square(lane % points, 2)[None, :]
    rows = square(jnp.arange(points, dtype=jnp.int32), 1)
    squares = plane[:, None, :] + rows[None, :, None]
    scale = -MIXING * 4.0 * math.pi / float(points**3)
    return scale / ((2.0 * math.pi / BOX_LENGTH) ** 2 * squares + SCREEN_SQ)


def owner_body(path_bands, occupied, path_kpts, mesh_kpts, mesh_shift):
    points = path_bands.shape[3]
    nbands = path_bands.shape[1]
    share = path_bands.shape[2]
    grid_count = lax.axis_size("grid")
    mesh_count = lax.axis_size("mesh")
    path_count = lax.axis_size("path")
    grid_index = lax.axis_index("grid")
    mesh_index = lax.axis_index("mesh")
    path_index = lax.axis_index("path")
    core = grid_index & 1
    z = grid_index >> 1
    nz = grid_count // 2
    column_bands = nbands // mesh_count
    rounds = column_bands // nz
    bands = path_bands[0]
    offsets = (2, 3, 1)

    def grid_swap(value, mask):
        return lax.ppermute(value, "grid", [(i, i ^ mask) for i in range(grid_count)])

    def axis_swap(value, axis, count):
        return lax.ppermute(value, axis, [(i, i ^ 1) for i in range(count)])

    piece = occupied[0, 0]
    got = {0: piece}
    for d in offsets:
        got[d] = grid_swap(piece, 2 * d)
    first = jnp.stack([got[0], got[1]])
    second = jnp.stack([got[2], got[3]])
    same = mesh_index == core

    def by_orbital(mine):
        theirs = axis_swap(mine, "mesh", mesh_count)
        kept = jnp.where(same, mine, theirs)
        crossed = grid_swap(jnp.where(same, theirs, mine), 1)
        return kept, crossed

    first_own = jnp.stack(by_orbital(first))
    first_far = axis_swap(first_own, "path", path_count)
    rows = jnp.stack([second, axis_swap(second, "path", path_count)])
    orbital = (first_own, first_far, *by_orbital(rows))

    mesh_point = lax.dynamic_index_in_dim(mesh_kpts, core, 0, keepdims=False)
    shift = lax.dynamic_index_in_dim(mesh_shift, core, 0, keepdims=False)
    kernel = owner_kernel_values(path_kpts[0], mesh_point, shift, points)
    spots = jnp.stack([z, core, path_index])

    received = []
    for turn in range(rounds):
        parts = [None] * nz
        for d in (0,) + offsets:
            at = mesh_index * column_bands + rounds * (z ^ d) + turn
            sent = lax.dynamic_index_in_dim(bands, at, 0, keepdims=False)
            parts[d] = grid_swap(sent, 2 * d) if d else sent
        received.append(parts)

    result = jnp.zeros((column_bands, share, points, 2 * points), jnp.float32)
    inner = jnp.zeros((2 * nbands, 2 * points), jnp.float32)
    for turn in range(rounds):
        mine = received[turn]
        other = [grid_swap(mine[d], 1) for d in range(nz)]
        keep, send = apply_pair(spots, mine, other, orbital, kernel)
        chunks = {}
        for d in offsets + (0,):
            chunk = keep[d] + grid_swap(send[d], 1)
            chunks[d] = grid_swap(chunk, 2 * d) if d else chunk
        for d in (0, 1, 2, 3):
            slot = rounds * (z ^ d) + turn
            result = lax.dynamic_update_index_in_dim(result, chunks[d], slot, 0)
            at = (mesh_index * column_bands + slot).reshape(1)
            inner = intersect(at, bands, chunks[d], inner)
    for bit in range(grid_count.bit_length() - 1):
        inner = inner + grid_swap(inner, 1 << bit)
    inner = inner + axis_swap(inner, "mesh", mesh_count)
    intersection = inner[:, :nbands].reshape(2, nbands, nbands) / float(points**3)
    return (result[None], intersection[None])


def owner_per_device(*operands):
    return owner_body(*operands)


def owner_fits(mesh, path_bands, occupied):
    paths, columns, planes = mesh.shape["path"], mesh.shape["mesh"], mesh.shape["grid"]
    points, nbands = path_bands.shape[3], path_bands.shape[1]
    orbitals = occupied.shape[0] * occupied.shape[1]
    return (
        paths == 2
        and columns == 2
        and planes == 8
        and path_bands.shape[0] == paths
        and occupied.shape[0] == columns
        and orbitals == columns
        and 2 * points == LANES
        and path_bands.shape[2] == points
        and nbands % (columns * planes // 2) == 0
        and points % (4 * planes) == 0
    )


def solution(mesh):
    def run(path_bands, occupied, path_kpts, mesh_kpts, mesh_shift):
        fits = owner_fits(mesh, path_bands, occupied)
        step = jax.shard_map(
            owner_per_device if fits else spread_per_device,
            mesh=mesh,
            in_specs=(
                P("path", None, "grid", None, None),
                P("mesh", None, "grid", "path", None),
                P("path", None),
                P(),
                P(),
            ),
            out_specs=(P("path", "mesh", "grid", None, None), P("path", None, None, None)),
            check_vma=False,
        )
        return step(path_bands, occupied, path_kpts, mesh_kpts, mesh_shift)

    return run
```

profile of v0, /device:TPU:0, one launch (start us, length us, event | category | flops | bytes accessed | tf_op | source)
XLA Modules:
  0.0 168.9 jit_solution(10587533475836336749)
XLA Ops:
  0.6 5.1 %collective-permute-start.12 = (f32[8,32,128]{2,1,0:T(8,128)}, f32[8,32,128]{2,1,0:T(8,128)S(1)}, u32[]{:S(2)}, u32[]{:S(2)}) collective-permute-start(f32[8,32,128]{2,1,0:T(8,128)} %bitcast.88), channel_id=1, source_target_pairs={{0,6},{1,7},{2,4},{3,5},{4,2},{5,3},{6,0},{7,1},{8,14},{9,15},{10,... | collective-permute-start | bytes 393224 | tf_op jit(solution)/shard_map/ppermute | solution.py:514
  6.4 2.6 %dynamic-slice_bitcast_fusion = (f32[8,64,128]{2,1,0:T(8,128)}, f32[8,64,128]{2,1,0:T(8,128)S(1)}, f32[8,64,128]{2,1,0:T(8,128)S(1)}, f32[8,64,128]{2,1,0:T(8,12...) fusion(f32[1,16,8,64,128]{4,3,2,1,0:T(8,128)} %param.9, ...), kind=kLoop, calls=%fused_computation.13 | loop fusion | bytes 4194336 | tf_op jit(solution)/shard_map/jit(dynamic_index_in_dim)/squeeze | solution.py:548
  9.0 3.7 %collective-permute-start.25 = (f32[8,64,128]{2,1,0:T(8,128)}, f32[8,64,128]{2,1,0:T(8,128)S(1)}, u32[]{:S(2)}, u32[]{:S(2)}) collective-permute-start(f32[8,64,128]{2,1,0:T(8,128)} %get-tuple-element.38), channel_id=1, source_target_pairs={{0,6},{1,7},{2,4},{3,5},{4,2},{5,3},{6,0},{7,1},{8,14},{9,15},{10,... | collective-permute-start | bytes 786440 | tf_op jit(solution)/shard_map/ppermute | solution.py:514
  12.8 3.8 %collective-permute-start.23 = (f32[8,64,128]{2,1,0:T(8,128)S(1)}, f32[8,64,128]{2,1,0:T(8,128)S(1)}, u32[]{:S(2)}, u32[]{:S(2)}) collective-permute-start(f32[8,64,128]{2,1,0:T(8,128)S(1)} %get-tuple-element.40), channel_id=1, source_target_pairs={{0,2},{1,3},{2,0},{3,1},{4,6},{5,7},{6,4},{7,5},{8,10},{9,11},{10,... | collective-permute-start | bytes 786440 | tf_op jit(solution)/shard_map/ppermute | solution.py:514
  16.6 12.6 %collective-permute-done.11 = f32[8,32,128]{2,1,0:T(8,128)S(1)} collective-permute-done((f32[8,32,128]{2,1,0:T(8,128)}, f32[8,32,128]{2,1,0:T(8,128)S(1)}, u32[]{:S(2)}, u32[]{:S(2)}) %collective-permute-start.11) | collective-permute-done | bytes 131104 | tf_op jit(solution)/shard_map/ppermute | solution.py:514
  29.3 1.6 collective-permute-start.13
  30.9 1.6 collective-permute-start.8
  33.7 2.1 %collective-permute-done.13 = f32[2,8,32,128]{3,2,1,0:T(8,128)S(1)} collective-permute-done((f32[2,8,32,128]{3,2,1,0:T(8,128)S(1)}, f32[2,8,32,128]{3,2,1,0:T(8,128)S(1)}, u32[]{:S(2)}, u32[]{:S(2)}) %collective-permute-start.13) | collective-permute-done | bytes 262176 | tf_op jit(solution)/shard_map/ppermute | solution.py:517
  35.8 1.5 collective-permute-start.14
  37.4 1.4 collective-permute-done.8
  38.9 1.2 fusion.12
  40.4 1.2 collective-permute-start.2
  41.9 3.1 %collective-permute-start = (f32[8,64,128]{2,1,0:T(8,128)}, f32[8,64,128]{2,1,0:T(8,128)}, u32[]{:S(2)}, u32[]{:S(2)}) collective-permute-start(f32[8,64,128]{2,1,0:T(8,128)} %get-tuple-element.44), channel_id=1, source_target_pairs={{0,2},{1,3},{2,0},{3,1},{4,6},{5,7},{6,4},{7,5},{8,10},{9,11},{10,... | collective-permute-start | bytes 786440 | tf_op jit(solution)/shard_map/ppermute | solution.py:514
  45.0 3.6 %collective-permute-done.14 = f32[2,2,8,32,128]{4,3,2,1,0:T(8,128)S(1)} collective-permute-done((f32[2,2,8,32,128]{4,3,2,1,0:T(8,128)S(1)}, f32[2,2,8,32,128]{4,3,2,1,0:T(8,128)S(1)}, u32[]{:S(2)}, u32[]{:S(2)}) %collective-permute-start.14) | collective-permute-done | bytes 524320 | tf_op jit(solution)/shard_map/ppermute | solution.py:517
  50.0 1.8 %collective-permute-done.2.refs_3_ = f32[8,64,128]{2,1,0:T(8,128)} collective-permute-done((f32[8,64,128]{2,1,0:T(8,128)}, f32[8,64,128]{2,1,0:T(8,128)}, u32[]{:S(2)}, u32[]{:S(2)}) %collective-permute-start.2) | collective-permute-done | bytes 262176 | tf_op jit(solution)/shard_map/ppermute | solution.py:514
  51.9 1.4 fusion.5
  53.3 11.2 %collective-permute-done.1.refs_2_ = f32[8,64,128]{2,1,0:T(8,128)} collective-permute-done((f32[8,64,128]{2,1,0:T(8,128)}, f32[8,64,128]{2,1,0:T(8,128)}, u32[]{:S(2)}, u32[]{:S(2)}) %collective-permute-start.1) | collective-permute-done | bytes 262176 | tf_op jit(solution)/shard_map/ppermute | solution.py:514
  65.7 1.3 fusion.16
  75.3 12.0 %pair.3 = (f32[8,64,128]{2,1,0:T(8,128)S(1)}, f32[8,64,128]{2,1,0:T(8,128)S(1)}, f32[8,64,128]{2,1,0:T(8,128)S(1)}, f32[8,64,128]{2,1,0:T(8,128)S(1)}, f32[8,64,...) custom-call(s32[3]{0:T(128)S(1)} %pad_add_fusion.spots_ref, ...), custom_call_target="tpu_custom_call" | custom-call | flops 2000000000 | bytes 7340032 | tf_op jit(solution)/shard_map/pair/pallas_call | solution.py:412
  89.6 11.7 %pair.2 = (f32[8,64,128]{2,1,0:T(8,128)S(1)}, f32[8,64,128]{2,1,0:T(8,128)S(1)}, f32[8,64,128]{2,1,0:T(8,128)S(1)}, f32[8,64,128]{2,1,0:T(8,128)S(1)}, f32[8,64,...) custom-call(s32[3]{0:T(128)S(1)} %pad_add_fusion.spots_ref, ...), custom_call_target="tpu_custom_call" | custom-call | flops 2000000000 | bytes 7340032 | tf_op jit(solution)/shard_map/pair/pallas_call | solution.py:412
  105.0 3.3 %collective-permute-start.20 = (f32[8,64,128]{2,1,0:T(8,128)S(1)}, f32[8,64,128]{2,1,0:T(8,128)S(1)}, u32[]{:S(2)}, u32[]{:S(2)}) collective-permute-start(f32[8,64,128]{2,1,0:T(8,128)S(1)} %add.357), channel_id=1, source_target_pairs={{0,4},{1,5},{2,6},{3,7},{4,0},{5,1},{6,2},{7,3},{8,12},{9,13},{10,... | collective-permute-start | bytes 786440 | tf_op jit(solution)/shard_map/ppermute | solution.py:514
  111.0 1.8 %collective-permute-start.34 = (f32[8,64,128]{2,1,0:T(8,128)S(1)}, f32[8,64,128]{2,1,0:T(8,128)S(1)}, u32[]{:S(2)}, u32[]{:S(2)}) collective-permute-start(f32[8,64,128]{2,1,0:T(8,128)S(1)} %add.375), channel_id=1, source_target_pairs={{0,4},{1,5},{2,6},{3,7},{4,0},{5,1},{6,2},{7,3},{8,12},{9,13},{10,... | collective-permute-start | bytes 786440 | tf_op jit(solution)/shard_map/ppermute | solution.py:514
  113.9 3.5 %collective-permute-done.18 = f32[8,64,128]{2,1,0:T(8,128)S(1)} collective-permute-done((f32[8,64,128]{2,1,0:T(8,128)S(1)}, f32[8,64,128]{2,1,0:T(8,128)S(1)}, u32[]{:S(2)}, u32[]{:S(2)}) %collective-permute-start.18) | collective-permute-done | bytes 262176 | tf_op jit(solution)/shard_map/ppermute | solution.py:514
  117.4 1.5 collective-permute-start.22
  118.9 2.3 %collective-permute-done.20 = f32[8,64,128]{2,1,0:T(8,128)S(1)} collective-permute-done((f32[8,64,128]{2,1,0:T(8,128)S(1)}, f32[8,64,128]{2,1,0:T(8,128)S(1)}, u32[]{:S(2)}, u32[]{:S(2)}) %collective-permute-start.20) | collective-permute-done | bytes 262176 | tf_op jit(solution)/shard_map/ppermute | solution.py:514
  121.2 2.4 %collective-permute-start.36 = (f32[8,64,128]{2,1,0:T(8,128)S(1)}, f32[8,64,128]{2,1,0:T(8,128)S(1)}, u32[]{:S(2)}, u32[]{:S(2)}) collective-permute-start(f32[8,64,128]{2,1,0:T(8,128)S(1)} %add.378), channel_id=1, source_target_pairs={{0,6},{1,7},{2,4},{3,5},{4,2},{5,3},{6,0},{7,1},{8,14},{9,15},{10,... | collective-permute-start | bytes 786440 | tf_op jit(solution)/shard_map/ppermute | solution.py:514
  123.6 12.8 %collective-permute-done.22 = f32[8,64,128]{2,1,0:T(8,128)S(1)} collective-permute-done((f32[8,64,128]{2,1,0:T(8,128)S(1)}, f32[8,64,128]{2,1,0:T(8,128)S(1)}, u32[]{:S(2)}, u32[]{:S(2)}) %collective-permute-start.22) | collective-permute-done | bytes 262176 | tf_op jit(solution)/shard_map/ppermute | solution.py:514
  141.5 2.1 %collective-permute-done.34 = f32[8,64,128]{2,1,0:T(8,128)S(1)} collective-permute-done((f32[8,64,128]{2,1,0:T(8,128)S(1)}, f32[8,64,128]{2,1,0:T(8,128)S(1)}, u32[]{:S(2)}, u32[]{:S(2)}) %collective-permute-start.34) | collective-permute-done | bytes 262176 | tf_op jit(solution)/shard_map/ppermute | solution.py:514
  146.9 11.3 %collective-permute-start.38 = (f32[32,128]{1,0:T(8,128)S(1)}, f32[32,128]{1,0:T(8,128)S(1)}, u32[]{:S(2)}, u32[]{:S(2)}) collective-permute-start(f32[32,128]{1,0:T(8,128)S(1)} %add.385), channel_id=1, source_target_pairs={{0,2},{1,3},{2,0},{3,1},{4,6},{5,7},{6,4},{7,5},{8,10},{9,11},{10,... | collective-permute-start | bytes 49160 | tf_op jit(solution)/shard_map/ppermute | solution.py:514
  159.9 2.9 %collective-permute-start.39 = (f32[32,128]{1,0:T(8,128)S(1)}, f32[32,128]{1,0:T(8,128)S(1)}, u32[]{:S(2)}, u32[]{:S(2)}) collective-permute-start(f32[32,128]{1,0:T(8,128)S(1)} %add.386), channel_id=1, source_target_pairs={{0,4},{1,5},{2,6},{3,7},{4,0},{5,1},{6,2},{7,3},{8,12},{9,13},{10,... | collective-permute-start | bytes 49160 | tf_op jit(solution)/shard_map/ppermute | solution.py:514
  164.5 1.7 %collective-permute-start.40 = (f32[32,128]{1,0:T(8,128)S(1)}, f32[32,128]{1,0:T(8,128)S(1)}, u32[]{:S(2)}, u32[]{:S(2)}) collective-permute-start(f32[32,128]{1,0:T(8,128)S(1)} %add.387), channel_id=1, source_target_pairs={{0,8},{8,0},{1,9},{9,1},{2,10},{10,2},{3,11},{11,3},{4,12},{12,4},... | collective-permute-start | bytes 49160 | tf_op jit(solution)/shard_map/ppermute | solution.py:517
  166.9 1.3 collective-permute-done.40
  (150 shorter events, 36.2 us)
Async XLA Ops:
  0.6 12.2 %collective-permute-start.12 = (f32[8,32,128]{2,1,0:T(8,128)}, f32[8,32,128]{2,1,0:T(8,128)S(1)}, u32[]{:S(2)}, u32[]{:S(2)}) collective-permute-start(f32[8,32,128]{2,1,0:T(8,128)} %bitcast.88), channel_id=1, source_target_pairs={{0,6},{1,7},{2,4},{3,5},{4,2},{5,3},{6,0},{7,1},{8,14},{9,15},{10,... | collective-permute-start | bytes 393224 | tf_op jit(solution)/shard_map/ppermute | solution.py:514
  5.8 23.5 %collective-permute-start.11 = (f32[8,32,128]{2,1,0:T(8,128)}, f32[8,32,128]{2,1,0:T(8,128)S(1)}, u32[]{:S(2)}, u32[]{:S(2)}) collective-permute-start(f32[8,32,128]{2,1,0:T(8,128)} %bitcast.89), channel_id=1, source_target_pairs={{0,4},{1,5},{2,6},{3,7},{4,0},{5,1},{6,2},{7,3},{8,12},{9,13},{10,... | collective-permute-start | bytes 393224 | tf_op jit(solution)/shard_map/ppermute | solution.py:514
  5.8 25.1 %collective-permute-start.7 = (f32[8,32,128]{2,1,0:T(8,128)}, f32[8,32,128]{2,1,0:T(8,128)S(1)}, u32[]{:S(2)}, u32[]{:S(2)}) collective-permute-start(f32[8,32,128]{2,1,0:T(8,128)} %bitcast.90), channel_id=1, source_target_pairs={{0,2},{1,3},{2,0},{3,1},{4,6},{5,7},{6,4},{7,5},{8,10},{9,11},{10,... | collective-permute-start | bytes 393224 | tf_op jit(solution)/shard_map/ppermute | solution.py:514
  9.0 32.7 %collective-permute-start.25 = (f32[8,64,128]{2,1,0:T(8,128)}, f32[8,64,128]{2,1,0:T(8,128)S(1)}, u32[]{:S(2)}, u32[]{:S(2)}) collective-permute-start(f32[8,64,128]{2,1,0:T(8,128)} %get-tuple-element.38), channel_id=1, source_target_pairs={{0,6},{1,7},{2,4},{3,5},{4,2},{5,3},{6,0},{7,1},{8,14},{9,15},{10,... | collective-permute-start | bytes 786440 | tf_op jit(solution)/shard_map/ppermute | solution.py:514
  12.8 29.1 %collective-permute-start.24 = (f32[8,64,128]{2,1,0:T(8,128)S(1)}, f32[8,64,128]{2,1,0:T(8,128)S(1)}, u32[]{:S(2)}, u32[]{:S(2)}) collective-permute-start(f32[8,64,128]{2,1,0:T(8,128)S(1)} %get-tuple-element.39), channel_id=1, source_target_pairs={{0,4},{1,5},{2,6},{3,7},{4,0},{5,1},{6,2},{7,3},{8,12},{9,13},{10,... | collective-permute-start | bytes 786440 | tf_op jit(solution)/shard_map/ppermute | solution.py:514
  12.8 36.7 %collective-permute-start.23 = (f32[8,64,128]{2,1,0:T(8,128)S(1)}, f32[8,64,128]{2,1,0:T(8,128)S(1)}, u32[]{:S(2)}, u32[]{:S(2)}) collective-permute-start(f32[8,64,128]{2,1,0:T(8,128)S(1)} %get-tuple-element.40), channel_id=1, source_target_pairs={{0,2},{1,3},{2,0},{3,1},{4,6},{5,7},{6,4},{7,5},{8,10},{9,11},{10,... | collective-permute-start | bytes 786440 | tf_op jit(solution)/shard_map/ppermute | solution.py:514
  29.3 6.5 %collective-permute-start.13 = (f32[2,8,32,128]{3,2,1,0:T(8,128)S(1)}, f32[2,8,32,128]{3,2,1,0:T(8,128)S(1)}, u32[]{:S(2)}, u32[]{:S(2)}) collective-permute-start(f32[2,8,32,128]{3,2,1,0:T(8,128)S(1)} %get-tuple-element.51), channel_id=1, source_target_pairs={{0,16},{16,0},{1,17},{17,1},{2,18},{18,2},{3,19},{19,3},{4,20},{20... | collective-permute-start | bytes 786440 | tf_op jit(solution)/shard_map/ppermute | solution.py:517
  30.9 7.9 %collective-permute-start.8 = (f32[2,8,32,128]{3,2,1,0:T(8,128)S(1)}, f32[2,8,32,128]{3,2,1,0:T(8,128)S(1)}, u32[]{:S(2)}, u32[]{:S(2)}) collective-permute-start(f32[2,8,32,128]{3,2,1,0:T(8,128)S(1)} %pad_maximum_fusion.2), channel_id=1, source_target_pairs={{0,8},{8,0},{1,9},{9,1},{2,10},{10,2},{3,11},{11,3},{4,12},{12,4},... | collective-permute-start | bytes 786440 | tf_op jit(solution)/shard_map/ppermute | solution.py:517
  35.8 12.7 %collective-permute-start.14 = (f32[2,2,8,32,128]{4,3,2,1,0:T(8,128)S(1)}, f32[2,2,8,32,128]{4,3,2,1,0:T(8,128)S(1)}, u32[]{:S(2)}, u32[]{:S(2)}) collective-permute-start(f32[2,2,8,32,128]{4,3,2,1,0:T(8,128)S(1)} %pad_maximum_fusion.1), channel_id=1, source_target_pairs={{0,8},{8,0},{1,9},{9,1},{2,10},{10,2},{3,11},{11,3},{4,12},{12,4},... | collective-permute-start | bytes 1572872 | tf_op jit(solution)/shard_map/ppermute | solution.py:517
  40.4 11.4 %collective-permute-start.2 = (f32[8,64,128]{2,1,0:T(8,128)}, f32[8,64,128]{2,1,0:T(8,128)}, u32[]{:S(2)}, u32[]{:S(2)}) collective-permute-start(f32[8,64,128]{2,1,0:T(8,128)} %get-tuple-element.42), channel_id=1, source_target_pairs={{0,6},{1,7},{2,4},{3,5},{4,2},{5,3},{6,0},{7,1},{8,14},{9,15},{10,... | collective-permute-start | bytes 786440 | tf_op jit(solution)/shard_map/ppermute | solution.py:514
  41.7 22.7 %collective-permute-start.1 = (f32[8,64,128]{2,1,0:T(8,128)}, f32[8,64,128]{2,1,0:T(8,128)}, u32[]{:S(2)}, u32[]{:S(2)}) collective-permute-start(f32[8,64,128]{2,1,0:T(8,128)} %get-tuple-element.43), channel_id=1, source_target_pairs={{0,4},{1,5},{2,6},{3,7},{4,0},{5,1},{6,2},{7,3},{8,12},{9,13},{10,... | collective-permute-start | bytes 786440 | tf_op jit(solution)/shard_map/ppermute | solution.py:514
  41.9 22.6 %collective-permute-start = (f32[8,64,128]{2,1,0:T(8,128)}, f32[8,64,128]{2,1,0:T(8,128)}, u32[]{:S(2)}, u32[]{:S(2)}) collective-permute-start(f32[8,64,128]{2,1,0:T(8,128)} %get-tuple-element.44), channel_id=1, source_target_pairs={{0,2},{1,3},{2,0},{3,1},{4,6},{5,7},{6,4},{7,5},{8,10},{9,11},{10,... | collective-permute-start | bytes 786440 | tf_op jit(solution)/shard_map/ppermute | solution.py:514
  48.6 16.4 %collective-permute-start.26 = (f32[8,64,128]{2,1,0:T(8,128)S(1)}, f32[8,64,128]{2,1,0:T(8,128)S(1)}, u32[]{:S(2)}, u32[]{:S(2)}) collective-permute-start(f32[8,64,128]{2,1,0:T(8,128)S(1)} %get-tuple-element.41.refs_0_), channel_id=1, source_target_pairs={{0,1},{1,0},{2,3},{3,2},{4,5},{5,4},{6,7},{7,6},{8,9},{9,8},{10,11... | collective-permute-start | bytes 786440 | tf_op jit(solution)/shard_map/ppermute | solution.py:514
  49.5 18.8 %collective-permute-start.10 = (f32[2,2,8,32,128]{4,3,2,1,0:T(8,128)S(1)}, f32[2,2,8,32,128]{4,3,2,1,0:T(8,128)S(1)}, u32[]{:S(2)}, u32[]{:S(2)}) collective-permute-start(f32[2,2,8,32,128]{4,3,2,1,0:T(8,128)S(1)} %pad_maximum_fusion.refs_8_), channel_id=1, source_target_pairs={{0,16},{16,0},{1,17},{17,1},{2,18},{18,2},{3,19},{19,3},{4,20},{20... | collective-permute-start | bytes 1572872 | tf_op jit(solution)/shard_map/ppermute | solution.py:517
  51.9 16.6 %collective-permute-start.15 = (f32[2,2,8,32,128]{4,3,2,1,0:T(8,128)}, f32[2,2,8,32,128]{4,3,2,1,0:T(8,128)S(1)}, u32[]{:S(2)}, u32[]{:S(2)}) collective-permute-start(f32[2,2,8,32,128]{4,3,2,1,0:T(8,128)} %get-tuple-element.46), channel_id=1, source_target_pairs={{0,1},{1,0},{2,3},{3,2},{4,5},{5,4},{6,7},{7,6},{8,9},{9,8},{10,11... | collective-permute-start | bytes 1572872 | tf_op jit(solution)/shard_map/ppermute | solution.py:514
  67.2 21.3 %collective-permute-start.3 = (f32[8,64,128]{2,1,0:T(8,128)S(1)}, f32[8,64,128]{2,1,0:T(8,128)S(1)}, u32[]{:S(2)}, u32[]{:S(2)}) collective-permute-start(f32[8,64,128]{2,1,0:T(8,128)S(1)} %get-tuple-element.45.refs_0_), channel_id=1, source_target_pairs={{0,1},{1,0},{2,3},{3,2},{4,5},{5,4},{6,7},{7,6},{8,9},{9,8},{10,11... | collective-permute-start | bytes 786440 | tf_op jit(solution)/shard_map/ppermute | solution.py:514
  67.8 20.7 %collective-permute-start.6 = (f32[8,64,128]{2,1,0:T(8,128)}, f32[8,64,128]{2,1,0:T(8,128)S(1)}, u32[]{:S(2)}, u32[]{:S(2)}) collective-permute-start(f32[8,64,128]{2,1,0:T(8,128)} %collective-permute-done.2.refs_3_), channel_id=1, source_target_pairs={{0,1},{1,0},{2,3},{3,2},{4,5},{5,4},{6,7},{7,6},{8,9},{9,8},{10,11... | collective-permute-start | bytes 786440 | tf_op jit(solution)/shard_map/ppermute | solution.py:514
  67.9 20.6 %collective-permute-start.5 = (f32[8,64,128]{2,1,0:T(8,128)}, f32[8,64,128]{2,1,0:T(8,128)S(1)}, u32[]{:S(2)}, u32[]{:S(2)}) collective-permute-start(f32[8,64,128]{2,1,0:T(8,128)} %collective-permute-done.1.refs_2_), channel_id=1, source_target_pairs={{0,1},{1,0},{2,3},{3,2},{4,5},{5,4},{6,7},{7,6},{8,9},{9,8},{10,11... | collective-permute-start | bytes 786440 | tf_op jit(solution)/shard_map/ppermute | solution.py:514
  68.3 20.2 %collective-permute-start.4 = (f32[8,64,128]{2,1,0:T(8,128)}, f32[8,64,128]{2,1,0:T(8,128)S(1)}, u32[]{:S(2)}, u32[]{:S(2)}) collective-permute-start(f32[8,64,128]{2,1,0:T(8,128)} %collective-permute-done.refs_1_), channel_id=1, source_target_pairs={{0,1},{1,0},{2,3},{3,2},{4,5},{5,4},{6,7},{7,6},{8,9},{9,8},{10,11... | collective-permute-start | bytes 786440 | tf_op jit(solution)/shard_map/ppermute | solution.py:514
  88.1 14.2 %collective-permute-start.31 = (f32[8,64,128]{2,1,0:T(8,128)S(1)}, f32[8,64,128]{2,1,0:T(8,128)S(1)}, u32[]{:S(2)}, u32[]{:S(2)}) collective-permute-start(f32[8,64,128]{2,1,0:T(8,128)S(1)} %get-tuple-element.29), channel_id=1, source_target_pairs={{0,1},{1,0},{2,3},{3,2},{4,5},{5,4},{6,7},{7,6},{8,9},{9,8},{10,11... | collective-permute-start | bytes 786440 | tf_op jit(solution)/shard_map/ppermute | solution.py:514
  101.9 7.9 %collective-permute-start.33 = (f32[8,64,128]{2,1,0:T(8,128)}, f32[8,64,128]{2,1,0:T(8,128)S(1)}, u32[]{:S(2)}, u32[]{:S(2)}) collective-permute-start(f32[8,64,128]{2,1,0:T(8,128)} %get-tuple-element.31), channel_id=1, source_target_pairs={{0,1},{1,0},{2,3},{3,2},{4,5},{5,4},{6,7},{7,6},{8,9},{9,8},{10,11... | collective-permute-start | bytes 786440 | tf_op jit(solution)/shard_map/ppermute | solution.py:514
  102.3 7.6 %collective-permute-start.35 = (f32[8,64,128]{2,1,0:T(8,128)}, f32[8,64,128]{2,1,0:T(8,128)}, u32[]{:S(2)}, u32[]{:S(2)}) collective-permute-start(f32[8,64,128]{2,1,0:T(8,128)} %get-tuple-element.33), channel_id=1, source_target_pairs={{0,1},{1,0},{2,3},{3,2},{4,5},{5,4},{6,7},{7,6},{8,9},{9,8},{10,11... | collective-permute-start | bytes 786440 | tf_op jit(solution)/shard_map/ppermute | solution.py:514
  102.9 8.2 %collective-permute-start.21 = (f32[8,64,128]{2,1,0:T(8,128)S(1)}, f32[8,64,128]{2,1,0:T(8,128)S(1)}, u32[]{:S(2)}, u32[]{:S(2)}) collective-permute-start(f32[8,64,128]{2,1,0:T(8,128)S(1)} %get-tuple-element.25), channel_id=1, source_target_pairs={{0,1},{1,0},{2,3},{3,2},{4,5},{5,4},{6,7},{7,6},{8,9},{9,8},{10,11... | collective-permute-start | bytes 786440 | tf_op jit(solution)/shard_map/ppermute | solution.py:514
  104.0 13.4 %collective-permute-start.18 = (f32[8,64,128]{2,1,0:T(8,128)S(1)}, f32[8,64,128]{2,1,0:T(8,128)S(1)}, u32[]{:S(2)}, u32[]{:S(2)}) collective-permute-start(f32[8,64,128]{2,1,0:T(8,128)S(1)} %add.355), channel_id=1, source_target_pairs={{0,2},{1,3},{2,0},{3,1},{4,6},{5,7},{6,4},{7,5},{8,10},{9,11},{10,... | collective-permute-start | bytes 786440 | tf_op jit(solution)/shard_map/ppermute | solution.py:514
  105.0 16.2 %collective-permute-start.20 = (f32[8,64,128]{2,1,0:T(8,128)S(1)}, f32[8,64,128]{2,1,0:T(8,128)S(1)}, u32[]{:S(2)}, u32[]{:S(2)}) collective-permute-start(f32[8,64,128]{2,1,0:T(8,128)S(1)} %add.357), channel_id=1, source_target_pairs={{0,4},{1,5},{2,6},{3,7},{4,0},{5,1},{6,2},{7,3},{8,12},{9,13},{10,... | collective-permute-start | bytes 786440 | tf_op jit(solution)/shard_map/ppermute | solution.py:514
  109.8 29.6 %collective-permute-start.30 = (f32[8,64,128]{2,1,0:T(8,128)S(1)}, f32[8,64,128]{2,1,0:T(8,128)S(1)}, u32[]{:S(2)}, u32[]{:S(2)}) collective-permute-start(f32[8,64,128]{2,1,0:T(8,128)S(1)} %copy-done.8), channel_id=1, source_target_pairs={{0,1},{1,0},{2,3},{3,2},{4,5},{5,4},{6,7},{7,6},{8,9},{9,8},{10,11... | collective-permute-start | bytes 786440 | tf_op jit(solution)/shard_map/ppermute | solution.py:514
  109.9 30.6 %collective-permute-start.32 = (f32[8,64,128]{2,1,0:T(8,128)S(1)}, f32[8,64,128]{2,1,0:T(8,128)S(1)}, u32[]{:S(2)}, u32[]{:S(2)}) collective-permute-start(f32[8,64,128]{2,1,0:T(8,128)S(1)} %add.372), channel_id=1, source_target_pairs={{0,2},{1,3},{2,0},{3,1},{4,6},{5,7},{6,4},{7,5},{8,10},{9,11},{10,... | collective-permute-start | bytes 786440 | tf_op jit(solution)/shard_map/ppermute | solution.py:514
  111.0 32.6 %collective-permute-start.34 = (f32[8,64,128]{2,1,0:T(8,128)S(1)}, f32[8,64,128]{2,1,0:T(8,128)S(1)}, u32[]{:S(2)}, u32[]{:S(2)}) collective-permute-start(f32[8,64,128]{2,1,0:T(8,128)S(1)} %add.375), channel_id=1, source_target_pairs={{0,4},{1,5},{2,6},{3,7},{4,0},{5,1},{6,2},{7,3},{8,12},{9,13},{10,... | collective-permute-start | bytes 786440 | tf_op jit(solution)/shard_map/ppermute | solution.py:514
  117.4 19.0 %collective-permute-start.22 = (f32[8,64,128]{2,1,0:T(8,128)S(1)}, f32[8,64,128]{2,1,0:T(8,128)S(1)}, u32[]{:S(2)}, u32[]{:S(2)}) collective-permute-start(f32[8,64,128]{2,1,0:T(8,128)S(1)} %add.359), channel_id=1, source_target_pairs={{0,6},{1,7},{2,4},{3,5},{4,2},{5,3},{6,0},{7,1},{8,14},{9,15},{10,... | collective-permute-start | bytes 786440 | tf_op jit(solution)/shard_map/ppermute | solution.py:514
  121.2 23.4 %collective-permute-start.36 = (f32[8,64,128]{2,1,0:T(8,128)S(1)}, f32[8,64,128]{2,1,0:T(8,128)S(1)}, u32[]{:S(2)}, u32[]{:S(2)}) collective-permute-start(f32[8,64,128]{2,1,0:T(8,128)S(1)} %add.378), channel_id=1, source_target_pairs={{0,6},{1,7},{2,4},{3,5},{4,2},{5,3},{6,0},{7,1},{8,14},{9,15},{10,... | collective-permute-start | bytes 786440 | tf_op jit(solution)/shard_map/ppermute | solution.py:514
  146.9 13.0 %collective-permute-start.38 = (f32[32,128]{1,0:T(8,128)S(1)}, f32[32,128]{1,0:T(8,128)S(1)}, u32[]{:S(2)}, u32[]{:S(2)}) collective-permute-start(f32[32,128]{1,0:T(8,128)S(1)} %add.385), channel_id=1, source_target_pairs={{0,2},{1,3},{2,0},{3,1},{4,6},{5,7},{6,4},{7,5},{8,10},{9,11},{10,... | collective-permute-start | bytes 49160 | tf_op jit(solution)/shard_map/ppermute | solution.py:514
  159.9 4.6 %collective-permute-start.39 = (f32[32,128]{1,0:T(8,128)S(1)}, f32[32,128]{1,0:T(8,128)S(1)}, u32[]{:S(2)}, u32[]{:S(2)}) collective-permute-start(f32[32,128]{1,0:T(8,128)S(1)} %add.386), channel_id=1, source_target_pairs={{0,4},{1,5},{2,6},{3,7},{4,0},{5,1},{6,2},{7,3},{8,12},{9,13},{10,... | collective-permute-start | bytes 49160 | tf_op jit(solution)/shard_map/ppermute | solution.py:514
  (35 other events, 234.1 us)
where the time goes:
time: 169 us
  waiting for transfers between devices  59 us (35%)
  starting transfers between devices  51.3 us (30%)
  Pallas kernels  31.8 us (19%)
  local copies, waits for them, and re-layouts  16.3 us (10%)
  other arithmetic  9.35 us (6%)
    ppermute x36, waiting for transfers between devices, grid_swap(): lax.ppermute(value, 'grid', [(i, i ^ mask) for i in range(grid_count)])  50.5 us
    ppermute x36, starting transfers between devices, grid_swap(): lax.ppermute(value, 'grid', [(i, i ^ mask) for i in range(grid_count)])  44.5 us
    pallas_call x2, Pallas kernels, apply_pair(): pl.pallas_call(pair_kernel, out_shape=(shape,) * (2 * count), in_specs=[p...  23.8 us
    unnamed x52, local copies, waits for them, and re-layouts  10.1 us
    ppermute x5, waiting for transfers between devices, axis_swap(): return lax.ppermute(value, axis, [(i, i ^ 1) for i in range(count)])  8.47 us
    pallas_call x8, Pallas kernels, intersect(): pl.pallas_call(intersect_kernel, out_shape=jax.ShapeDtypeStruct((2 * nban...  8.02 us
    ppermute x5, starting transfers between devices, axis_swap(): return lax.ppermute(value, axis, [(i, i ^ 1) for i in range(count)])  6.89 us
  transfers between devices with their start and end apart: 41, of which 17 were waited for; matrix products, arithmetic and copies ran while one was open for 9% of the time, Pallas kernels for 18%

commit v1 on v0

--- a/solution.py
+++ b/solution.py
@@ -277,26 +277,31 @@
     nz = 4
     mine, other = refs[:nz], refs[nz : 2 * nz]
     first_own, first_far, second_kept, second_crossed = refs[2 * nz : 2 * nz + 4]
-    kern_ref, table_ref, tw_ref = refs[2 * nz + 4 : 2 * nz + 7]
+    kern_ref, tw_ref, table_hbm = refs[2 * nz + 4 : 2 * nz + 7]
+    keep, send = refs[2 * nz + 7 : 3 * nz + 7], refs[3 * nz + 7 : 4 * nz + 7]
+    vre, vim, table_ref, sem = refs[4 * nz + 7 :]
+    copy = pltpu.make_async_copy(table_hbm, table_ref, sem)
+    copy.start()
     lfh, lfl, lih, lil, rf, ri = [table_ref.at[at] for at in range(6)]
-    keep, send = refs[2 * nz + 7 : 3 * nz + 7], refs[3 * nz + 7 : 4 * nz + 7]
-    vre, vim = refs[4 * nz + 7 :]
     share, rows, lanes = mine[0].shape
     points = rows
     half_z = nz // 2
     z, core, path = spots_ref[0], spots_ref[1], spots_ref[2]
     low = lax.broadcasted_iota(jnp.int32, (rows, lanes), 1) < points
-    step = 4
+    step = 8
 
     def swap(v):
         return pltpu.roll(v, points, v.ndim - 1)
 
     def orbital(d, parity, i):
-        if d < half_z:
-            own, far = first_own[parity, d, i], first_far[parity, d, i]
+        at = d // 2
+        if d % 2 == 0:
+            own, far = first_own[parity, at, i], first_far[parity, at, i]
         else:
             ref = second_crossed if parity else second_kept
-            own, far = ref[0, d - half_z, i], ref[1, d - half_z, i]
+            r = jnp.concatenate([ref[path, at, i], ref[1 - path, at, i]], 0)
+            s = swap(r)
+            return jnp.where(low, r, s), jnp.where(low, s, -r)
         r = jnp.concatenate([jnp.where(path == 0, own, far), jnp.where(path == 0, far, own)], 0)
         s = swap(r)
         return jnp.where(low, r, s), jnp.where(low, s, -r)
@@ -365,6 +370,7 @@
 
         lax.fori_loop(0, share // step, body, 0)
 
+    copy.wait()
     each_part(forward)
 
     n = vre.shape[0]
@@ -407,20 +413,24 @@
     last, row, tw = transform_tables(rows)
     shape = jax.ShapeDtypeStruct(mine[0].shape, jnp.float32)
     vm = pl.BlockSpec(memory_space=pltpu.VMEM)
-    operands = [*mine, *other, *orbital, kern, np.stack(last + row), tw]
+    table = jnp.asarray(np.stack(last + row))
+    operands = [*mine, *other, *orbital, kern, tw]
     count = len(mine)
     outs = pl.pallas_call(
         pair_kernel,
         out_shape=(shape,) * (2 * count),
-        in_specs=[pl.BlockSpec(memory_space=pltpu.SMEM)] + [vm] * len(operands),
+        in_specs=[pl.BlockSpec(memory_space=pltpu.SMEM)]
+        + [vm] * len(operands)
+        + [pl.BlockSpec(memory_space=pltpu.HBM)],
         out_specs=(vm,) * (2 * count),
-        scratch_shapes=[pltpu.VMEM((count * share, rows, lanes), jnp.float32)] * 2,
+        scratch_shapes=[pltpu.VMEM((count * share, rows, lanes), jnp.float32)] * 2
+        + [pltpu.VMEM(table.shape, table.dtype), pltpu.SemaphoreType.DMA],
         cost_estimate=pl.CostEstimate(
             flops=2 * 10**9, bytes_accessed=7 * 2**20, transcendentals=0
         ),
         compiler_params=pltpu.CompilerParams(vmem_limit_bytes=30 * 2**20),
         name="pair",
-    )(spots, *operands)
+    )(spots, *operands, table)
     return outs[:count], outs[count:]
 
 
@@ -517,18 +527,14 @@
         return lax.ppermute(value, axis, [(i, i ^ 1) for i in range(count)])
 
     piece = occupied[0, 0]
-    got = {0: piece}
-    for d in offsets:
-        got[d] = grid_swap(piece, 2 * d)
-    first = jnp.stack([got[0], got[1]])
-    second = jnp.stack([got[2], got[3]])
+    first = jnp.stack([piece, grid_swap(piece, 2 * 2)])
+    second = grid_swap(first, 2)
     same = mesh_index == core
 
     def by_orbital(mine):
         theirs = axis_swap(mine, "mesh", mesh_count)
-        kept = jnp.where(same, mine, theirs)
-        crossed = grid_swap(jnp.where(same, theirs, mine), 1)
-        return kept, crossed
+        kept, crossed = jnp.where(same, mine, theirs), jnp.where(same, theirs, mine)
+        return kept, grid_swap(crossed, 1)
 
     first_own = jnp.stack(by_orbital(first))
     first_far = axis_swap(first_own, "path", path_count)
@@ -557,16 +563,23 @@
         keep, send = apply_pair(spots, mine, other, orbital, kernel)
         chunks = {}
         for d in offsets + (0,):
-            chunk = keep[d] + grid_swap(send[d], 1)
+            crossed = grid_swap(send[d], 1)
+            chunk = keep[d] + crossed
             chunks[d] = grid_swap(chunk, 2 * d) if d else chunk
         for d in (0, 1, 2, 3):
             slot = rounds * (z ^ d) + turn
             result = lax.dynamic_update_index_in_dim(result, chunks[d], slot, 0)
             at = (mesh_index * column_bands + slot).reshape(1)
             inner = intersect(at, bands, chunks[d], inner)
-    for bit in range(grid_count.bit_length() - 1):
-        inner = inner + grid_swap(inner, 1 << bit)
-    inner = inner + axis_swap(inner, "mesh", mesh_count)
+
+    def chip_swap(value, mask):
+        axes, count = ("mesh", "grid"), mesh_count * grid_count
+        return lax.ppermute(value, axes, [(i, i ^ mask) for i in range(count)])
+
+    far = [grid_swap(inner, 2 * d) for d in (3, 2, 1)]
+    inner = (inner + far[2]) + (far[0] + far[1])
+    near = [chip_swap(inner, mask) for mask in (grid_count, grid_count + 1, 1)]
+    inner = (inner + near[2]) + (near[0] + near[1])
     intersection = inner[:, :nbands].reshape(2, nbands, nbands) / float(points**3)
     return (result[None], intersection[None])
 

time: 169 us -> 166 us (0.982)
  waiting for transfers between devices: 59 us -> 53.3 us
  starting transfers between devices: 51.3 us -> 55.7 us
  Pallas kernels: 31.8 us -> 28.6 us
  other arithmetic: 9.35 us -> 12.3 us
  local copies, waits for them, and re-layouts: 16.3 us -> 13.8 us
    ppermute x5 -> x4, waiting for transfers between devices: 8.47 us -> 3.01 us  [axis_swap(): return lax.ppermute(value, axis, [(i, i ^ 1) for i in range(count)])]
    pallas_call x2, Pallas kernels: 23.8 us -> 20.6 us  [apply_pair(): pl.pallas_call(pair_kernel, out_shape=(shape,) * (2 * count), in_specs=[p...]
    ppermute x36 -> x35, starting transfers between devices: 44.5 us -> 47.6 us  [grid_swap(): lax.ppermute(value, 'grid', [(i, i ^ mask) for i in range(grid_count)])]
    ppermute x36 -> x35, waiting for transfers between devices: 50.5 us -> 48.4 us  [grid_swap(): lax.ppermute(value, 'grid', [(i, i ^ mask) for i in range(grid_count)])]
    dynamic_update_slice x6, local copies, waits for them, and re-layouts: 2.22 us -> 0.13 us  [owner_body(): result = lax.dynamic_update_index_in_dim(result, chunks[d], slot, 0)]
    ppermute x0 -> x3, waiting for transfers between devices: none -> 1.92 us  [chip_swap(): return lax.ppermute(value, axes, [(i, i ^ mask) for i in range(count)])]
    ppermute x0 -> x3, starting transfers between devices: none -> 1.92 us  [chip_swap(): return lax.ppermute(value, axes, [(i, i ^ mask) for i in range(count)])]
    ppermute x5 -> x4, starting transfers between devices: 6.89 us -> 6.21 us  [axis_swap(): return lax.ppermute(value, axis, [(i, i ^ 1) for i in range(count)])]
  transfers between devices with their start and end apart: 41 -> 42, of which waited for: 17 -> 16; matrix products, arithmetic and copies ran while one was open for 9% -> 9% of each run, Pallas kernels for 18% -> 17%
where the time goes in v1:
time: 166 us; the launch traced here: 165 us
  starting transfers between devices  55.7 us (34%)
  waiting for transfers between devices  53.3 us (32%)
  Pallas kernels  28.6 us (17%)
  local copies, waits for them, and re-layouts  13.8 us (8%)
  other arithmetic  12.3 us (7%)
    ppermute x35, waiting for transfers between devices, grid_swap(): lax.ppermute(value, 'grid', [(i, i ^ mask) for i in range(grid_count)])  48.4 us
    ppermute x35, starting transfers between devices, grid_swap(): lax.ppermute(value, 'grid', [(i, i ^ mask) for i in range(grid_count)])  47.6 us
    pallas_call x2, Pallas kernels, apply_pair(): pl.pallas_call(pair_kernel, out_shape=(shape,) * (2 * count), in_specs=[p...  20.6 us
    unnamed x54, local copies, waits for them, and re-layouts  9.5 us
    pallas_call x8, Pallas kernels, intersect(): pl.pallas_call(intersect_kernel, out_shape=jax.ShapeDtypeStruct((2 * nban...  8.01 us
    ppermute x4, starting transfers between devices, axis_swap(): return lax.ppermute(value, axis, [(i, i ^ 1) for i in range(count)])  6.21 us
  transfers between devices with their start and end apart: 42, of which 16 were waited for; matrix products, arithmetic and copies ran while one was open for 9% of the time, Pallas kernels for 17%

profile of v1, /device:TPU:0, one launch (start us, length us, event | category | flops | bytes accessed | tf_op | source)
XLA Modules:
  0.0 164.9 jit_solution(8139985639001086231)
XLA Ops:
  0.6 4.1 %collective-permute-start.7 = (f32[8,32,128]{2,1,0:T(8,128)}, f32[8,32,128]{2,1,0:T(8,128)S(1)}, u32[]{:S(2)}, u32[]{:S(2)}) collective-permute-start(f32[8,32,128]{2,1,0:T(8,128)} %bitcast.87), channel_id=1, source_target_pairs={{0,4},{1,5},{2,6},{3,7},{4,0},{5,1},{6,2},{7,3},{8,12},{9,13},{10,... | collective-permute-start | bytes 393224 | tf_op jit(solution)/shard_map/ppermute | solution.py:524
  4.8 6.5 %collective-permute-done.7 = f32[8,32,128]{2,1,0:T(8,128)S(1)} collective-permute-done((f32[8,32,128]{2,1,0:T(8,128)}, f32[8,32,128]{2,1,0:T(8,128)S(1)}, u32[]{:S(2)}, u32[]{:S(2)}) %collective-permute-start.7) | collective-permute-done | bytes 131104 | tf_op jit(solution)/shard_map/ppermute | solution.py:524
  13.2 2.6 %dynamic-slice_bitcast_fusion = (f32[8,64,128]{2,1,0:T(8,128)}, f32[8,64,128]{2,1,0:T(8,128)S(1)}, f32[8,64,128]{2,1,0:T(8,128)}, f32[8,64,128]{2,1,0:T(8,128)S(...) fusion(f32[1,16,8,64,128]{4,3,2,1,0:T(8,128)} %param.9, ...), kind=kLoop, calls=%fused_computation.12 | loop fusion | bytes 4194336 | tf_op jit(solution)/shard_map/jit(dynamic_index_in_dim)/squeeze | solution.py:554
  15.7 2.7 %collective-permute-start.24 = (f32[8,64,128]{2,1,0:T(8,128)}, f32[8,64,128]{2,1,0:T(8,128)S(1)}, u32[]{:S(2)}, u32[]{:S(2)}) collective-permute-start(f32[8,64,128]{2,1,0:T(8,128)} %get-tuple-element.38), channel_id=1, source_target_pairs={{0,6},{1,7},{2,4},{3,5},{4,2},{5,3},{6,0},{7,1},{8,14},{9,15},{10,... | collective-permute-start | bytes 786440 | tf_op jit(solution)/shard_map/ppermute | solution.py:524
  19.0 1.1 collective-permute-start.22
  20.1 1.6 collective-permute-start.12
  21.7 1.6 collective-permute-start.8
  24.6 2.7 %collective-permute-done.12 = f32[2,8,32,128]{3,2,1,0:T(8,128)S(1)} collective-permute-done((f32[2,8,32,128]{3,2,1,0:T(8,128)S(1)}, f32[2,8,32,128]{3,2,1,0:T(8,128)S(1)}, u32[]{:S(2)}, u32[]{:S(2)}) %collective-permute-start.12) | collective-permute-done | bytes 262176 | tf_op jit(solution)/shard_map/ppermute | solution.py:527
  27.3 1.6 collective-permute-start.13
  30.4 1.4 fusion.13
  31.9 10.8 %collective-permute-start.2 = (f32[8,64,128]{2,1,0:T(8,128)}, f32[8,64,128]{2,1,0:T(8,128)}, u32[]{:S(2)}, u32[]{:S(2)}) collective-permute-start(f32[8,64,128]{2,1,0:T(8,128)} %get-tuple-element.42), channel_id=1, source_target_pairs={{0,6},{1,7},{2,4},{3,5},{4,2},{5,3},{6,0},{7,1},{8,14},{9,15},{10,... | collective-permute-start | bytes 786440 | tf_op jit(solution)/shard_map/ppermute | solution.py:524
  44.4 1.5 collective-permute-start.10
  45.8 4.5 %collective-permute-done.2.refs_3_ = f32[8,64,128]{2,1,0:T(8,128)} collective-permute-done((f32[8,64,128]{2,1,0:T(8,128)}, f32[8,64,128]{2,1,0:T(8,128)}, u32[]{:S(2)}, u32[]{:S(2)}) %collective-permute-start.2) | collective-permute-done | bytes 262176 | tf_op jit(solution)/shard_map/ppermute | solution.py:524
  50.3 1.4 fusion.5
  51.7 13.8 %collective-permute-done.1.refs_2_ = f32[8,64,128]{2,1,0:T(8,128)} collective-permute-done((f32[8,64,128]{2,1,0:T(8,128)}, f32[8,64,128]{2,1,0:T(8,128)}, u32[]{:S(2)}, u32[]{:S(2)}) %collective-permute-start.1) | collective-permute-done | bytes 262176 | tf_op jit(solution)/shard_map/ppermute | solution.py:524
  67.4 1.3 fusion.17
  71.0 1.0 copy-done.5
  75.9 1.1 copy-done.19
  77.0 10.6 %pair.3 = (f32[8,64,128]{2,1,0:T(8,128)S(1)}, f32[8,64,128]{2,1,0:T(8,128)S(1)}, f32[8,64,128]{2,1,0:T(8,128)S(1)}, f32[8,64,128]{2,1,0:T(8,128)S(1)}, f32[8,64,...) custom-call(s32[3]{0:T(128)S(1)} %pad_add_fusion.spots_ref, ...), custom_call_target="tpu_custom_call" | custom-call | flops 2000000000 | bytes 7340032 | tf_op jit(solution)/shard_map/pair/pallas_call | solution.py:419
  89.5 10.1 %pair.2 = (f32[8,64,128]{2,1,0:T(8,128)S(1)}, f32[8,64,128]{2,1,0:T(8,128)S(1)}, f32[8,64,128]{2,1,0:T(8,128)S(1)}, f32[8,64,128]{2,1,0:T(8,128)S(1)}, f32[8,64,...) custom-call(s32[3]{0:T(128)S(1)} %pad_add_fusion.spots_ref, ...), custom_call_target="tpu_custom_call" | custom-call | flops 2000000000 | bytes 7340032 | tf_op jit(solution)/shard_map/pair/pallas_call | solution.py:419
  102.1 2.9 %collective-permute-start.19 = (f32[8,64,128]{2,1,0:T(8,128)S(1)}, f32[8,64,128]{2,1,0:T(8,128)S(1)}, u32[]{:S(2)}, u32[]{:S(2)}) collective-permute-start(f32[8,64,128]{2,1,0:T(8,128)S(1)} %add.363), channel_id=1, source_target_pairs={{0,4},{1,5},{2,6},{3,7},{4,0},{5,1},{6,2},{7,3},{8,12},{9,13},{10,... | collective-permute-start | bytes 786440 | tf_op jit(solution)/shard_map/ppermute | solution.py:524
  105.3 1.2 bitcast_dynamic-update-slice_fusion.7
  109.1 1.5 collective-permute-start.33
  112.6 3.5 %collective-permute-done.17 = f32[8,64,128]{2,1,0:T(8,128)S(1)} collective-permute-done((f32[8,64,128]{2,1,0:T(8,128)S(1)}, f32[8,64,128]{2,1,0:T(8,128)S(1)}, u32[]{:S(2)}, u32[]{:S(2)}) %collective-permute-start.17) | collective-permute-done | bytes 262176 | tf_op jit(solution)/shard_map/ppermute | solution.py:524
  116.1 1.2 collective-permute-start.21
  117.8 2.8 %collective-permute-start.35 = (f32[8,64,128]{2,1,0:T(8,128)S(1)}, f32[8,64,128]{2,1,0:T(8,128)S(1)}, u32[]{:S(2)}, u32[]{:S(2)}) collective-permute-start(f32[8,64,128]{2,1,0:T(8,128)S(1)} %add.384), channel_id=1, source_target_pairs={{0,6},{1,7},{2,4},{3,5},{4,2},{5,3},{6,0},{7,1},{8,14},{9,15},{10,... | collective-permute-start | bytes 786440 | tf_op jit(solution)/shard_map/ppermute | solution.py:524
  120.6 13.5 %collective-permute-done.21 = f32[8,64,128]{2,1,0:T(8,128)S(1)} collective-permute-done((f32[8,64,128]{2,1,0:T(8,128)S(1)}, f32[8,64,128]{2,1,0:T(8,128)S(1)}, u32[]{:S(2)}, u32[]{:S(2)}) %collective-permute-start.21) | collective-permute-done | bytes 262176 | tf_op jit(solution)/shard_map/ppermute | solution.py:524
  142.2 12.6 %collective-permute-start.38 = (f32[32,128]{1,0:T(8,128)S(1)}, f32[32,128]{1,0:T(8,128)S(1)}, u32[]{:S(2)}, u32[]{:S(2)}) collective-permute-start(f32[32,128]{1,0:T(8,128)S(1)} %intersect.15), channel_id=1, source_target_pairs={{0,4},{1,5},{2,6},{3,7},{4,0},{5,1},{6,2},{7,3},{8,12},{9,13},{10,... | collective-permute-start | bytes 49160 | tf_op jit(solution)/shard_map/ppermute | solution.py:524
  154.9 1.0 collective-permute-start.37
  156.6 3.8 %collective-permute-done.37 = f32[32,128]{1,0:T(8,128)S(1)} collective-permute-done((f32[32,128]{1,0:T(8,128)S(1)}, f32[32,128]{1,0:T(8,128)S(1)}, u32[]{:S(2)}, u32[]{:S(2)}) %collective-permute-start.37) | collective-permute-done | bytes 16416 | tf_op jit(solution)/shard_map/ppermute | solution.py:524
  160.5 1.6 collective-permute-start.40
  162.4 1.4 collective-permute-done.41
  (151 shorter events, 34.8 us)
Async XLA Ops:
  0.6 10.6 %collective-permute-start.7 = (f32[8,32,128]{2,1,0:T(8,128)}, f32[8,32,128]{2,1,0:T(8,128)S(1)}, u32[]{:S(2)}, u32[]{:S(2)}) collective-permute-start(f32[8,32,128]{2,1,0:T(8,128)} %bitcast.87), channel_id=1, source_target_pairs={{0,4},{1,5},{2,6},{3,7},{4,0},{5,1},{6,2},{7,3},{8,12},{9,13},{10,... | collective-permute-start | bytes 393224 | tf_op jit(solution)/shard_map/ppermute | solution.py:524
  12.3 7.9 %collective-permute-start.11 = (f32[2,8,32,128]{3,2,1,0:T(8,128)S(1)}, f32[2,8,32,128]{3,2,1,0:T(8,128)S(1)}, u32[]{:S(2)}, u32[]{:S(2)}) collective-permute-start(f32[2,8,32,128]{3,2,1,0:T(8,128)S(1)} %pad_maximum_fusion.2), channel_id=1, source_target_pairs={{0,2},{1,3},{2,0},{3,1},{4,6},{5,7},{6,4},{7,5},{8,10},{9,11},{10,... | collective-permute-start | bytes 786440 | tf_op jit(solution)/shard_map/ppermute | solution.py:524
  15.7 27.0 %collective-permute-start.24 = (f32[8,64,128]{2,1,0:T(8,128)}, f32[8,64,128]{2,1,0:T(8,128)S(1)}, u32[]{:S(2)}, u32[]{:S(2)}) collective-permute-start(f32[8,64,128]{2,1,0:T(8,128)} %get-tuple-element.38), channel_id=1, source_target_pairs={{0,6},{1,7},{2,4},{3,5},{4,2},{5,3},{6,0},{7,1},{8,14},{9,15},{10,... | collective-permute-start | bytes 786440 | tf_op jit(solution)/shard_map/ppermute | solution.py:524
  18.5 24.4 %collective-permute-start.23 = (f32[8,64,128]{2,1,0:T(8,128)S(1)}, f32[8,64,128]{2,1,0:T(8,128)S(1)}, u32[]{:S(2)}, u32[]{:S(2)}) collective-permute-start(f32[8,64,128]{2,1,0:T(8,128)S(1)} %get-tuple-element.39), channel_id=1, source_target_pairs={{0,4},{1,5},{2,6},{3,7},{4,0},{5,1},{6,2},{7,3},{8,12},{9,13},{10,... | collective-permute-start | bytes 786440 | tf_op jit(solution)/shard_map/ppermute | solution.py:524
  19.0 25.3 %collective-permute-start.22 = (f32[8,64,128]{2,1,0:T(8,128)}, f32[8,64,128]{2,1,0:T(8,128)S(1)}, u32[]{:S(2)}, u32[]{:S(2)}) collective-permute-start(f32[8,64,128]{2,1,0:T(8,128)} %get-tuple-element.40), channel_id=1, source_target_pairs={{0,2},{1,3},{2,0},{3,1},{4,6},{5,7},{6,4},{7,5},{8,10},{9,11},{10,... | collective-permute-start | bytes 786440 | tf_op jit(solution)/shard_map/ppermute | solution.py:524
  20.1 7.2 %collective-permute-start.12 = (f32[2,8,32,128]{3,2,1,0:T(8,128)S(1)}, f32[2,8,32,128]{3,2,1,0:T(8,128)S(1)}, u32[]{:S(2)}, u32[]{:S(2)}) collective-permute-start(f32[2,8,32,128]{3,2,1,0:T(8,128)S(1)} %collective-permute-done.11), channel_id=1, source_target_pairs={{0,16},{16,0},{1,17},{17,1},{2,18},{18,2},{3,19},{19,3},{4,20},{20... | collective-permute-start | bytes 786440 | tf_op jit(solution)/shard_map/ppermute | solution.py:527
  21.7 7.5 %collective-permute-start.8 = (f32[2,8,32,128]{3,2,1,0:T(8,128)S(1)}, f32[2,8,32,128]{3,2,1,0:T(8,128)}, u32[]{:S(2)}, u32[]{:S(2)}) collective-permute-start(f32[2,8,32,128]{3,2,1,0:T(8,128)S(1)} %pad_maximum_fusion.2), channel_id=1, source_target_pairs={{0,8},{8,0},{1,9},{9,1},{2,10},{10,2},{3,11},{11,3},{4,12},{12,4},... | collective-permute-start | bytes 786440 | tf_op jit(solution)/shard_map/ppermute | solution.py:527
  27.3 16.0 %collective-permute-start.13 = (f32[2,2,8,32,128]{4,3,2,1,0:T(8,128)S(1)}, f32[2,2,8,32,128]{4,3,2,1,0:T(8,128)S(1)}, u32[]{:S(2)}, u32[]{:S(2)}) collective-permute-start(f32[2,2,8,32,128]{4,3,2,1,0:T(8,128)S(1)} %pad_maximum_fusion.1), channel_id=1, source_target_pairs={{0,8},{8,0},{1,9},{9,1},{2,10},{10,2},{3,11},{11,3},{4,12},{12,4},... | collective-permute-start | bytes 1572872 | tf_op jit(solution)/shard_map/ppermute | solution.py:527
  31.9 18.4 %collective-permute-start.2 = (f32[8,64,128]{2,1,0:T(8,128)}, f32[8,64,128]{2,1,0:T(8,128)}, u32[]{:S(2)}, u32[]{:S(2)}) collective-permute-start(f32[8,64,128]{2,1,0:T(8,128)} %get-tuple-element.42), channel_id=1, source_target_pairs={{0,6},{1,7},{2,4},{3,5},{4,2},{5,3},{6,0},{7,1},{8,14},{9,15},{10,... | collective-permute-start | bytes 786440 | tf_op jit(solution)/shard_map/ppermute | solution.py:524
  42.7 22.8 %collective-permute-start.1 = (f32[8,64,128]{2,1,0:T(8,128)}, f32[8,64,128]{2,1,0:T(8,128)}, u32[]{:S(2)}, u32[]{:S(2)}) collective-permute-start(f32[8,64,128]{2,1,0:T(8,128)} %get-tuple-element.43), channel_id=1, source_target_pairs={{0,4},{1,5},{2,6},{3,7},{4,0},{5,1},{6,2},{7,3},{8,12},{9,13},{10,... | collective-permute-start | bytes 786440 | tf_op jit(solution)/shard_map/ppermute | solution.py:524
  42.8 22.7 %collective-permute-start = (f32[8,64,128]{2,1,0:T(8,128)}, f32[8,64,128]{2,1,0:T(8,128)S(1)}, u32[]{:S(2)}, u32[]{:S(2)}) collective-permute-start(f32[8,64,128]{2,1,0:T(8,128)} %get-tuple-element.44), channel_id=1, source_target_pairs={{0,2},{1,3},{2,0},{3,1},{4,6},{5,7},{6,4},{7,5},{8,10},{9,11},{10,... | collective-permute-start | bytes 786440 | tf_op jit(solution)/shard_map/ppermute | solution.py:524
  43.4 22.7 %collective-permute-start.25 = (f32[8,64,128]{2,1,0:T(8,128)S(1)}, f32[8,64,128]{2,1,0:T(8,128)S(1)}, u32[]{:S(2)}, u32[]{:S(2)}) collective-permute-start(f32[8,64,128]{2,1,0:T(8,128)S(1)} %get-tuple-element.41.refs_0_), channel_id=1, source_target_pairs={{0,1},{1,0},{2,3},{3,2},{4,5},{5,4},{6,7},{7,6},{8,9},{9,8},{10,11... | collective-permute-start | bytes 786440 | tf_op jit(solution)/shard_map/ppermute | solution.py:524
  44.4 25.3 %collective-permute-start.10 = (f32[2,2,8,32,128]{4,3,2,1,0:T(8,128)S(1)}, f32[2,2,8,32,128]{4,3,2,1,0:T(8,128)S(1)}, u32[]{:S(2)}, u32[]{:S(2)}) collective-permute-start(f32[2,2,8,32,128]{4,3,2,1,0:T(8,128)S(1)} %pad_maximum_fusion.refs_8_), channel_id=1, source_target_pairs={{0,16},{16,0},{1,17},{17,1},{2,18},{18,2},{3,19},{19,3},{4,20},{20... | collective-permute-start | bytes 1572872 | tf_op jit(solution)/shard_map/ppermute | solution.py:527
  50.3 19.9 %collective-permute-start.14 = (f32[2,2,8,32,128]{4,3,2,1,0:T(8,128)}, f32[2,2,8,32,128]{4,3,2,1,0:T(8,128)S(1)}, u32[]{:S(2)}, u32[]{:S(2)}) collective-permute-start(f32[2,2,8,32,128]{4,3,2,1,0:T(8,128)} %get-tuple-element.46), channel_id=1, source_target_pairs={{0,1},{1,0},{2,3},{3,2},{4,5},{5,4},{6,7},{7,6},{8,9},{9,8},{10,11... | collective-permute-start | bytes 1572872 | tf_op jit(solution)/shard_map/ppermute | solution.py:524
  69.0 19.4 %collective-permute-start.3 = (f32[8,64,128]{2,1,0:T(8,128)S(1)}, f32[8,64,128]{2,1,0:T(8,128)S(1)}, u32[]{:S(2)}, u32[]{:S(2)}) collective-permute-start(f32[8,64,128]{2,1,0:T(8,128)S(1)} %get-tuple-element.45.refs_0_), channel_id=1, source_target_pairs={{0,1},{1,0},{2,3},{3,2},{4,5},{5,4},{6,7},{7,6},{8,9},{9,8},{10,11... | collective-permute-start | bytes 786440 | tf_op jit(solution)/shard_map/ppermute | solution.py:524
  69.1 19.3 %collective-permute-start.6 = (f32[8,64,128]{2,1,0:T(8,128)}, f32[8,64,128]{2,1,0:T(8,128)S(1)}, u32[]{:S(2)}, u32[]{:S(2)}) collective-permute-start(f32[8,64,128]{2,1,0:T(8,128)} %collective-permute-done.2.refs_3_), channel_id=1, source_target_pairs={{0,1},{1,0},{2,3},{3,2},{4,5},{5,4},{6,7},{7,6},{8,9},{9,8},{10,11... | collective-permute-start | bytes 786440 | tf_op jit(solution)/shard_map/ppermute | solution.py:524
  69.6 18.9 %collective-permute-start.5 = (f32[8,64,128]{2,1,0:T(8,128)}, f32[8,64,128]{2,1,0:T(8,128)S(1)}, u32[]{:S(2)}, u32[]{:S(2)}) collective-permute-start(f32[8,64,128]{2,1,0:T(8,128)} %collective-permute-done.1.refs_2_), channel_id=1, source_target_pairs={{0,1},{1,0},{2,3},{3,2},{4,5},{5,4},{6,7},{7,6},{8,9},{9,8},{10,11... | collective-permute-start | bytes 786440 | tf_op jit(solution)/shard_map/ppermute | solution.py:524
  69.7 18.8 %collective-permute-start.4 = (f32[8,64,128]{2,1,0:T(8,128)}, f32[8,64,128]{2,1,0:T(8,128)S(1)}, u32[]{:S(2)}, u32[]{:S(2)}) collective-permute-start(f32[8,64,128]{2,1,0:T(8,128)} %copy-done.15), channel_id=1, source_target_pairs={{0,1},{1,0},{2,3},{3,2},{4,5},{5,4},{6,7},{7,6},{8,9},{9,8},{10,11... | collective-permute-start | bytes 786440 | tf_op jit(solution)/shard_map/ppermute | solution.py:524
  88.3 12.3 %collective-permute-start.30 = (f32[8,64,128]{2,1,0:T(8,128)S(1)}, f32[8,64,128]{2,1,0:T(8,128)S(1)}, u32[]{:S(2)}, u32[]{:S(2)}) collective-permute-start(f32[8,64,128]{2,1,0:T(8,128)S(1)} %get-tuple-element.29), channel_id=1, source_target_pairs={{0,1},{1,0},{2,3},{3,2},{4,5},{5,4},{6,7},{7,6},{8,9},{9,8},{10,11... | collective-permute-start | bytes 786440 | tf_op jit(solution)/shard_map/ppermute | solution.py:524
  100.6 6.0 %collective-permute-start.32 = (f32[8,64,128]{2,1,0:T(8,128)}, f32[8,64,128]{2,1,0:T(8,128)}, u32[]{:S(2)}, u32[]{:S(2)}) collective-permute-start(f32[8,64,128]{2,1,0:T(8,128)} %get-tuple-element.31), channel_id=1, source_target_pairs={{0,1},{1,0},{2,3},{3,2},{4,5},{5,4},{6,7},{7,6},{8,9},{9,8},{10,11... | collective-permute-start | bytes 786440 | tf_op jit(solution)/shard_map/ppermute | solution.py:524
  100.7 7.0 %collective-permute-start.34 = (f32[8,64,128]{2,1,0:T(8,128)}, f32[8,64,128]{2,1,0:T(8,128)}, u32[]{:S(2)}, u32[]{:S(2)}) collective-permute-start(f32[8,64,128]{2,1,0:T(8,128)} %get-tuple-element.33), channel_id=1, source_target_pairs={{0,1},{1,0},{2,3},{3,2},{4,5},{5,4},{6,7},{7,6},{8,9},{9,8},{10,11... | collective-permute-start | bytes 786440 | tf_op jit(solution)/shard_map/ppermute | solution.py:524
  101.2 7.8 %collective-permute-start.20 = (f32[8,64,128]{2,1,0:T(8,128)S(1)}, f32[8,64,128]{2,1,0:T(8,128)}, u32[]{:S(2)}, u32[]{:S(2)}) collective-permute-start(f32[8,64,128]{2,1,0:T(8,128)S(1)} %get-tuple-element.25), channel_id=1, source_target_pairs={{0,1},{1,0},{2,3},{3,2},{4,5},{5,4},{6,7},{7,6},{8,9},{9,8},{10,11... | collective-permute-start | bytes 786440 | tf_op jit(solution)/shard_map/ppermute | solution.py:524
  101.7 14.4 %collective-permute-start.17 = (f32[8,64,128]{2,1,0:T(8,128)S(1)}, f32[8,64,128]{2,1,0:T(8,128)S(1)}, u32[]{:S(2)}, u32[]{:S(2)}) collective-permute-start(f32[8,64,128]{2,1,0:T(8,128)S(1)} %add.361), channel_id=1, source_target_pairs={{0,2},{1,3},{2,0},{3,1},{4,6},{5,7},{6,4},{7,5},{8,10},{9,11},{10,... | collective-permute-start | bytes 786440 | tf_op jit(solution)/shard_map/ppermute | solution.py:524
  102.1 15.7 %collective-permute-start.19 = (f32[8,64,128]{2,1,0:T(8,128)S(1)}, f32[8,64,128]{2,1,0:T(8,128)S(1)}, u32[]{:S(2)}, u32[]{:S(2)}) collective-permute-start(f32[8,64,128]{2,1,0:T(8,128)S(1)} %add.363), channel_id=1, source_target_pairs={{0,4},{1,5},{2,6},{3,7},{4,0},{5,1},{6,2},{7,3},{8,12},{9,13},{10,... | collective-permute-start | bytes 786440 | tf_op jit(solution)/shard_map/ppermute | solution.py:524
  106.5 30.6 %collective-permute-start.29 = (f32[8,64,128]{2,1,0:T(8,128)S(1)}, f32[8,64,128]{2,1,0:T(8,128)S(1)}, u32[]{:S(2)}, u32[]{:S(2)}) collective-permute-start(f32[8,64,128]{2,1,0:T(8,128)S(1)} %copy-done.8), channel_id=1, source_target_pairs={{0,1},{1,0},{2,3},{3,2},{4,5},{5,4},{6,7},{7,6},{8,9},{9,8},{10,11... | collective-permute-start | bytes 786440 | tf_op jit(solution)/shard_map/ppermute | solution.py:524
  107.6 30.6 %collective-permute-start.31 = (f32[8,64,128]{2,1,0:T(8,128)S(1)}, f32[8,64,128]{2,1,0:T(8,128)S(1)}, u32[]{:S(2)}, u32[]{:S(2)}) collective-permute-start(f32[8,64,128]{2,1,0:T(8,128)S(1)} %add.378), channel_id=1, source_target_pairs={{0,2},{1,3},{2,0},{3,1},{4,6},{5,7},{6,4},{7,5},{8,10},{9,11},{10,... | collective-permute-start | bytes 786440 | tf_op jit(solution)/shard_map/ppermute | solution.py:524
  109.1 31.2 %collective-permute-start.33 = (f32[8,64,128]{2,1,0:T(8,128)S(1)}, f32[8,64,128]{2,1,0:T(8,128)S(1)}, u32[]{:S(2)}, u32[]{:S(2)}) collective-permute-start(f32[8,64,128]{2,1,0:T(8,128)S(1)} %add.381), channel_id=1, source_target_pairs={{0,4},{1,5},{2,6},{3,7},{4,0},{5,1},{6,2},{7,3},{8,12},{9,13},{10,... | collective-permute-start | bytes 786440 | tf_op jit(solution)/shard_map/ppermute | solution.py:524
  116.1 18.1 %collective-permute-start.21 = (f32[8,64,128]{2,1,0:T(8,128)S(1)}, f32[8,64,128]{2,1,0:T(8,128)S(1)}, u32[]{:S(2)}, u32[]{:S(2)}) collective-permute-start(f32[8,64,128]{2,1,0:T(8,128)S(1)} %add.365), channel_id=1, source_target_pairs={{0,6},{1,7},{2,4},{3,5},{4,2},{5,3},{6,0},{7,1},{8,14},{9,15},{10,... | collective-permute-start | bytes 786440 | tf_op jit(solution)/shard_map/ppermute | solution.py:524
  117.8 23.4 %collective-permute-start.35 = (f32[8,64,128]{2,1,0:T(8,128)S(1)}, f32[8,64,128]{2,1,0:T(8,128)S(1)}, u32[]{:S(2)}, u32[]{:S(2)}) collective-permute-start(f32[8,64,128]{2,1,0:T(8,128)S(1)} %add.384), channel_id=1, source_target_pairs={{0,6},{1,7},{2,4},{3,5},{4,2},{5,3},{6,0},{7,1},{8,14},{9,15},{10,... | collective-permute-start | bytes 786440 | tf_op jit(solution)/shard_map/ppermute | solution.py:524
  142.2 14.3 %collective-permute-start.38 = (f32[32,128]{1,0:T(8,128)S(1)}, f32[32,128]{1,0:T(8,128)S(1)}, u32[]{:S(2)}, u32[]{:S(2)}) collective-permute-start(f32[32,128]{1,0:T(8,128)S(1)} %intersect.15), channel_id=1, source_target_pairs={{0,4},{1,5},{2,6},{3,7},{4,0},{5,1},{6,2},{7,3},{8,12},{9,13},{10,... | collective-permute-start | bytes 49160 | tf_op jit(solution)/shard_map/ppermute | solution.py:524
  154.9 5.5 %collective-permute-start.37 = (f32[32,128]{1,0:T(8,128)S(1)}, f32[32,128]{1,0:T(8,128)S(1)}, u32[]{:S(2)}, u32[]{:S(2)}) collective-permute-start(f32[32,128]{1,0:T(8,128)S(1)} %intersect.15), channel_id=1, source_target_pairs={{0,6},{1,7},{2,4},{3,5},{4,2},{5,3},{6,0},{7,1},{8,14},{9,15},{10,... | collective-permute-start | bytes 49160 | tf_op jit(solution)/shard_map/ppermute | solution.py:524
  155.9 4.5 %collective-permute-start.36 = (f32[32,128]{1,0:T(8,128)S(1)}, f32[32,128]{1,0:T(8,128)S(1)}, u32[]{:S(2)}, u32[]{:S(2)}) collective-permute-start(f32[32,128]{1,0:T(8,128)S(1)} %intersect.15), channel_id=1, source_target_pairs={{0,2},{1,3},{2,0},{3,1},{4,6},{5,7},{6,4},{7,5},{8,10},{9,11},{10,... | collective-permute-start | bytes 49160 | tf_op jit(solution)/shard_map/ppermute | solution.py:524
  (37 other events, 258.6 us)
